TPU v7x, 128 devices: a whole 4x4x4 slice. The times are simulated.
128 devices in a mesh: occ: 8 (over y, core), vir: 16 (over x, z).
Axes of the slice: x: 4, y: 4, z: 4, core: 2. Of those that a mesh axis runs over, the one named last changes fastest.
Arguments:
- amplitudes: bfloat16 [4096, 49152], P('occ', 'vir'), may hold values from -6 to 6
- integral_tiles: bfloat16 [16, 256, 128, 128], P('vir', 'occ'), may hold values from -0.0625 to 0.0625
- tile_cd: int32 [16, 256], replicated, may hold values from 0 to 23, as said below
- tile_ab: int32 [16, 256], replicated, may hold values from 0 to 63, as said below
- slot_tile: int32 [64], replicated, may hold values from 0 to 63, as said below
- residual_in: float32 [4096, 8192], P('occ', 'vir'), may hold values from -6 to 6
- occ_level: float32 [4096], P('occ'), may hold values from -3 to -1
- vir_level: float32 [8192], P('vir'), may hold values from 0.5 to 3
Outputs:
- update: float32 [4096, 8192], P('occ', 'vir')
Inputs may be any that keep to these rules, and one draw needn't show every extreme that they name: `tile_cd`: within a group no pair of contracted tile and slab tile repeats. `tile_ab`: for every group and every index w of vir, the group's tiles name slab tiles held in exactly 2 of the slots w * 4 to (w + 1) * 4 - 1. `slot_tile`: A permutation of the slab tiles.
All inputs are finite; a program needn't handle non-finite values.
Results may differ from a plain program's by a relative error of at most 0.0003.
Values may be sent and summed in bfloat16 or wider, within the bound.
A program may use at most 128 MiB of HBM per device.

v0:
```python
import jax
import jax.numpy as jnp
from jax import lax
from jax.sharding import PartitionSpec as P

CAP = 2


def slot_numbers(ab_tiles, slot_tile):
    match = ab_tiles[..., None] == slot_tile
    places = lax.broadcasted_iota(jnp.int32, match.shape, match.ndim - 1)
    return jnp.sum(jnp.where(match, places, 0), axis=-1)


def shards(
    amplitudes, integral_tiles, tile_cd, tile_ab, slot_tile, residual_in, occ_level, vir_level
):
    groups = lax.axis_size("vir")
    mine = lax.axis_index("vir")
    rows = amplitudes.shape[0]
    tile = integral_tiles.shape[-1]
    kind_count = amplitudes.shape[1] // tile
    total_slots = slot_tile.shape[0]
    per_owner = total_slots // groups
    slots_all = slot_numbers(tile_ab, slot_tile)
    every_slot = jnp.arange(total_slots, dtype=jnp.int32)
    reached = jnp.any(slots_all[..., None] == every_slot, axis=1).astype(jnp.int32)
    reached = reached.reshape(groups, groups, per_owner)
    rank = jnp.cumsum(reached, axis=-1) - 1
    picks = jnp.arange(CAP, dtype=jnp.int32)
    hit = (reached[..., None] == 1) & (rank[..., None] == picks)
    within = lax.broadcasted_iota(jnp.int32, hit.shape, 2)
    chosen = jnp.sum(jnp.where(hit, within, 0), axis=2)
    my_kinds = lax.dynamic_index_in_dim(tile_cd, mine, 0, keepdims=False)
    my_slots = lax.dynamic_index_in_dim(slots_all, mine, 0, keepdims=False)
    my_chosen = lax.dynamic_index_in_dim(chosen, mine, 0, keepdims=False)
    owner_of = my_slots // per_owner
    inside = my_slots % per_owner
    candidates = jnp.take(my_chosen, owner_of, axis=0)
    match = candidates == inside[:, None]
    cap_iota = lax.broadcasted_iota(jnp.int32, match.shape, 1)
    column_of = owner_of * CAP + jnp.sum(jnp.where(match, cap_iota, 0), axis=1)
    empty = jnp.zeros((groups * CAP, kind_count, tile, tile), jnp.bfloat16)
    weight = empty.at[column_of, my_kinds].set(
        lax.all_gather(integral_tiles, "occ", axis=1, tiled=True)[0]
    )
    left = amplitudes.reshape(rows, kind_count, tile)
    partial_value = jnp.einsum("rkt,ckts->rcs", left, weight, preferred_element_type=jnp.float32)
    owner_base = jnp.arange(groups, dtype=jnp.int32)[:, None] * per_owner
    places = (owner_base + my_chosen).reshape(-1)
    placing = (places[:, None] == every_slot[None, :]).astype(jnp.float32)
    spread = jnp.einsum("rcs,cq->rqs", partial_value, placing, precision=lax.Precision.HIGHEST)
    summed = lax.psum_scatter(spread, "vir", scatter_dimension=1, tiled=True)
    by_slot = summed.reshape(rows, per_owner * tile)
    return (residual_in + by_slot) / (occ_level[:, None] - vir_level[None, :])


def solution(mesh):
    in_specs = (
        P("occ", "vir"),
        P("vir", "occ", None, None),
        P(),
        P(),
        P(),
        P("occ", "vir"),
        P("occ"),
        P("vir"),
    )
    out_specs = P("occ", "vir")
    return jax.shard_map(shards, mesh=mesh, in_specs=in_specs, out_specs=out_specs, check_vma=False)
```

profile of v0, /device:TPU:1, one launch (start us, length us, event | category | flops | bytes accessed | tf_op | source)
XLA Modules:
  0.0 295.7 jit_solution(15879185883777184707)
XLA Ops:
  6.5 0.7 all-gather.2.cloned.1.call-update
  7.3 1.1 select_reduce_fusion
  8.4 0.4 fusion.2
  8.8 0.1 copy.35
  9.0 0.1 copy.36
  9.2 0.1 copy.38
  9.3 0.1 copy.39
  9.4 0.1 squeeze.18
  9.5 0.1 add.113
  9.7 0.7 gather_fusion
  10.4 0.2 select_reduce_fusion.1
  10.6 0.7 or_select_fusion
  11.4 51.0 %all-gather.2.cloned.1.call-done = bf16[1,256,128,128]{3,2,0,1:T(8,128)(2,1)} async-done(((bf16[1,32,128,128]{3,2,0,1:T(8,128)(2,1)}), bf16[1,256,128,128]{3,2,0,1:T(8,128)(2,1)}) %all-gather.2.cloned.1.call-update) | async-done | bytes 8388624 | tf_op jit(solution)/shard_map/all_gather | solution.py:45
  62.4 8.8 %broadcast_in_dim.40 = bf16[32,24,128,128]{3,2,1,0:T(8,128)(2,1)} broadcast(bf16[]{:T(256)} %constant.68.clone.1), dimensions={} | broadcast | bytes 25165826 | tf_op jit(solution)/shard_map/broadcast_in_dim | solution.py:43
  71.2 39.9 %scatter_fusion = bf16[32,24,128,128]{3,2,1,0:T(8,128)(2,1)} fusion(bf16[32,24,128,128]{3,2,1,0:T(8,128)(2,1)} %broadcast_in_dim.40, s32[256]{0:T(256)S(1)} %bitcast.45, bf16[256,128,128]{2,1,0:T(8,128)(2,1)} %bitcast.46), kind=kCustom, calls=%fused_computation.1 | custom fusion | bytes 25167872 | tf_op jit(solution)/shard_map/scatter | solution.py:44
  111.1 20.1 %convolution_bitcast_fusion.1 = f32[512,32,128]{0,2,1:T(8,128)} fusion(bf16[32,24,128,128]{3,2,1,0:T(8,128)(2,1)} %scatter_fusion, bf16[512,3072]{1,0:T(8,128)(2,1)S(1)} %copy-done), kind=kOutput, calls=%fused_computation.3 | convolution fusion | flops 12884901888 | bytes 36700160 | tf_op jit(solution)/shard_map/rkt,ckts->rcs/dot_general | solution.py:48
  131.2 10.3 %copy.43 = f32[512,32,128]{2,1,0:T(8,128)} copy(f32[512,32,128]{0,2,1:T(8,128)} %convolution_bitcast_fusion.1) | data formatting | bytes 16777216 | tf_op jit(solution)/shard_map/rkt,ckts->rcs/dot_general | solution.py:48
  141.5 9.4 %convolution_bitcast_fusion = f32[512,64,128]{2,1,0:T(8,128)S(1)} fusion(f32[512,32,128]{2,1,0:T(8,128)} %copy.43, s32[32]{0:T(128)S(1)} %add.115), kind=kOutput, calls=%fused_computation.2 | convolution fusion | flops 1610614784 | bytes 25165952 | tf_op jit(solution)/shard_map/rcs,cq->rqs/dot_general | solution.py:52
  150.9 19.5 %copy.44 = f32[512,64,128]{2,0,1:T(8,128)} copy(f32[512,64,128]{2,1,0:T(8,128)S(1)} %convolution_bitcast_fusion) | data formatting | bytes 33554432 | tf_op jit(solution)/shard_map/rcs,cq->rqs/transpose | solution.py:52
  170.4 2.7 copy.46
  173.1 107.9 %reduce-scatter.2.cloned.1.call-done = f32[512,4,128]{2,0,1:T(8,128)} async-done(((f32[512,64,128]{2,0,1:T(8,128)}), f32[512,4,128]{2,0,1:T(8,128)}) %reduce-scatter.2.cloned.1.call-update) | async-done | bytes 1048592 | tf_op jit(solution)/shard_map/reduce_scatter | solution.py:53
  281.0 2.5 copy.45
  283.5 2.8 fusion.1
  286.3 2.5 copy.47
  (25 shorter events, 0.4 us)
Async XLA Ops:
  6.5 104.6 %copy-start = (bf16[512,3072]{1,0:T(8,128)(2,1)S(1)}, bf16[512,3072]{1,0:T(8,128)(2,1)}, u32[]{:S(2)}) copy-start(bf16[512,3072]{1,0:T(8,128)(2,1)} %param.8) | copy-start | bytes 9437188
  6.5 55.8 %all-gather.2.cloned.1.call-start = ((), (), s32[]{:S(2)}) async-start(), calls=%async_computation.1 | async-start | bytes 9437184 | tf_op jit(solution)/shard_map/all_gather | solution.py:45
  7.3 273.7 %reduce-scatter.2.cloned.1.call-start = ((), (), s32[]{:S(2)}) async-start(), calls=%async_computation.2 | async-start | bytes 17825792 | tf_op jit(solution)/shard_map/reduce_scatter | solution.py:53
  170.4 113.1 %copy-start.2 = (f32[512]{0:T(512)S(1)}, f32[512]{0:T(512)}, u32[]{:S(2)}) copy-start(f32[512]{0:T(512)} %param.15) | copy-start | bytes 6148
  170.4 113.1 %copy-start.3 = (f32[512]{0:T(512)S(1)}, f32[512]{0:T(512)}, u32[]{:S(2)}) copy-start(f32[512]{0:T(512)} %param.14) | copy-start | bytes 6148
  170.4 118.4 %copy-start.1 = (bf16[512,3072]{1,0:T(8,128)(2,1)S(1)}, bf16[512,3072]{1,0:T(8,128)(2,1)}, u32[]{:S(2)}) copy-start(bf16[512,3072]{1,0:T(8,128)(2,1)} %param.8) | copy-start | bytes 9437188
Sparse Core Ops, SparseCore 0:
  9.0 53.2 all-gather.1
  170.5 110.3 reduce-scatter.1
where the time goes:
time: 297 us; the launch traced here: 296 us
  waiting for transfers between devices  160 us (54%)
  local copies, waits for them, and re-layouts  87.7 us (30%)
  matrix products  29.5 us (10%)
  between operations  13.5 us (5%)
  other arithmetic  5.33 us (2%)
    reduce_scatter x1, waiting for transfers between devices, shards(): summed = lax.psum_scatter(spread, 'vir', scatter_dimension=1, tiled=True)  108 us
    all_gather x1, waiting for transfers between devices, shards(): lax.all_gather(integral_tiles, 'occ', axis=1, tiled=True)[0]  51 us
    scatter x1, local copies, waits for them, and re-layouts, shards(): empty.at[column_of, my_kinds]  39.9 us
    dot_general x1, matrix products, shards(): jnp.einsum('rkt,ckts->rcs', left, weight, preferred_element_type=jnp.floa...  20.1 us
    transpose x1, local copies, waits for them, and re-layouts, shards(): jnp.einsum('rcs,cq->rqs', partial_value, placing, precision=lax.Precision...  19.5 us
    dot_general x1, local copies, waits for them, and re-layouts, shards(): jnp.einsum('rkt,ckts->rcs', left, weight, preferred_element_type=jnp.floa...  10.3 us
    dot_general x1, matrix products, shards(): jnp.einsum('rcs,cq->rqs', partial_value, placing, precision=lax.Precision...  9.42 us
    broadcast_in_dim x1, local copies, waits for them, and re-layouts, shards(): empty = jnp.zeros((groups * CAP, kind_count, tile, tile), jnp.bfloat16)  8.84 us
  transfers between devices with their start and end apart: 2, of which 2 were waited for; matrix products, arithmetic and copies ran while one was open for 2% of the time, Pallas kernels for 0%

commit v1 on v0

v1 whole, which is shorter than its diff:
```python
import jax
import jax.numpy as jnp
from jax import lax
from jax.experimental import pallas as pl
from jax.experimental.pallas import tpu as pltpu
from jax.sharding import PartitionSpec as P

CAP = 2
TILE = 128
MESH = pl.DeviceIdType.MESH
PIECES = 4
FULL = 32767.0

ORDER = (
    (2, 2), (2, 1), (1, 2), (2, 3), (3, 2), (2, 0), (0, 2), (1, 1),
    (3, 3), (1, 3), (3, 1), (1, 0), (3, 0), (0, 1), (0, 3), (0, 0),
)


def pick(i, values):
    out = jnp.int32(values[0])
    for n, v in enumerate(values[1:], 1):
        out = jnp.where(i == n, jnp.int32(v), out)
    return out


def code(v):
    top = jnp.maximum(jnp.max(jnp.abs(v), axis=0, keepdims=True), 1e-30)
    return jnp.round(v * (FULL / top)).astype(jnp.int32).astype(jnp.int16), top * (1.0 / FULL)


def kernel(
    table, chosen, amp_hbm, tiles_hbm, out,
    amp, pool, q1s, u1s, q1r, u1r, q2s, u2s, q2r, u2r, own, total,
    amp_sem, local_sem, gs_send, gs_recv, q1_send, q1_recv, u1_send, u1_recv, q2_send, q2_recv, u2_send, u2_recv,
):
    occ, vir = lax.axis_index("occ"), lax.axis_index("vir")
    y, core = occ // 2, occ % 2
    x, z = vir // 4, vir % 4
    up = (((y + 1) % 4) * 2 + core, vir)
    down = (((y + 3) % 4) * 2 + core, vir)
    mate = (y * 2 + 1 - core, vir)
    at_x = [(occ, ((x + d) % 4) * 4 + z) for d in range(4)]
    at_z = [(occ, x * 4 + (z + d) % 4) for d in range(4)]
    own_tiles = tiles_hbm.shape[0]
    part = own_tiles // PIECES
    kinds = amp_hbm.shape[1] // TILE
    half = amp_hbm.shape[0] // 2

    load_amp = pltpu.make_async_copy(amp_hbm, amp, amp_sem)
    load_amp.start()

    barrier = pltpu.get_barrier_semaphore()
    greeted = [up, down, mate] + at_x[1:] + at_z[1:]
    for other in greeted:
        pl.semaphore_signal(barrier, inc=1, device_id=other, device_id_type=MESH)
    pl.semaphore_wait(barrier, len(greeted))

    def place(yy, cc, piece):
        return pool.at[pl.ds(((yy % 4) * 2 + cc) * own_tiles + piece * part, part)]

    def mine(piece):
        return tiles_hbm.at[pl.ds(piece * part, part)]

    def send(kind, piece, source, target, device):
        return pltpu.make_async_remote_copy(
            src_ref=source, dst_ref=target, send_sem=gs_send.at[kind, piece],
            recv_sem=gs_recv.at[kind, piece], device_id=device, device_id_type=MESH,
        )

    pieces = range(PIECES)
    low, high = pieces[: PIECES // 2], pieces[PIECES // 2 :]
    first_up = [send(0, p, mine(p), place(y, core, p), up) for p in pieces]
    first_down = [send(1, p, mine(p), place(y, core, p), down) for p in pieces]
    to_mate = [send(3, p, mine(p), place(y, core, p), mate) for p in pieces]
    here = [pltpu.make_async_copy(mine(p), place(y, core, p), local_sem.at[p]) for p in pieces]
    for a, b in zip(pieces, list(high) + list(low)):
        first_up[a].start()
        first_down[b].start()
    for p in pieces:
        to_mate[p].start()
        here[p].start()
    pool[pool.shape[0] - 1] = jnp.zeros((TILE, TILE), pool.dtype)
    passed, relayed = {}, {}

    def relay(kind, p, yy):
        relayed[kind, p] = send(kind, p, place(yy, core, p), place(yy, core, p), mate)
        relayed[kind, p].start()

    for a, b in zip(pieces, list(high) + list(low)):
        first_up[a].wait_recv()
        if a in low:
            passed[a] = send(2, a, place(y + 3, core, a), place(y + 3, core, a), up)
            passed[a].start()
        first_down[b].wait_recv()
        if b in high:
            passed[b] = send(2, b, place(y + 1, core, b), place(y + 1, core, b), down)
            passed[b].start()
        relay(4, a, y + 3)
        relay(5, b, y + 1)
    for a, b in zip(low, high):
        for p in (a, b):
            passed[p].wait_recv()
            relay(6, p, y + 2)
    load_amp.wait()
    for p in pieces:
        here[p].wait()
        to_mate[p].wait_recv()
        relayed[4, p].wait_recv()
        relayed[5, p].wait_recv()
    for a, b in zip(low, high):
        relayed[6, a].wait_recv()
        relayed[6, b].wait_recv()

    def first_leg(h, d, e):
        device = (occ, ((x + d) % 4) * 4 + z) if h == 0 else (occ, x * 4 + (z + d) % 4)
        return [
            pltpu.make_async_remote_copy(
                src_ref=s.at[h, d, e], dst_ref=r.at[h, d, e], send_sem=ss.at[h, d, e],
                recv_sem=rs.at[h, d, e], device_id=device, device_id_type=MESH,
            )
            for s, r, ss, rs in ((q1s, q1r, q1_send, q1_recv), (u1s, u1r, u1_send, u1_recv))
        ]

    rows4 = lax.broadcasted_iota(jnp.int32, (4, TILE), 0)

    def one_owner(i, carry):
        dx, dz = pick(i, [o[0] for o in ORDER]), pick(i, [o[1] for o in ORDER])
        owner = ((x + dx) % 4) * 4 + (z + dz) % 4
        places = [chosen[owner * CAP + b] for b in range(CAP)]
        starts = [(owner * 4 + place) * kinds for place in places]
        value = jnp.zeros((2 * half, CAP * TILE), jnp.float32)
        for k in range(0, kinds, 2):
            rhs = jnp.concatenate(
                [
                    jnp.concatenate([pool[table[starts[b] + kk]] for b in range(CAP)], axis=1)
                    for kk in (k, k + 1)
                ],
                axis=0,
            )
            value = value + jnp.dot(
                amp[:, k * TILE : (k + 2) * TILE], rhs, preferred_element_type=jnp.float32
            )
        for h, d, e in ((0, dx, dz), (1, dz, dx)):
            units = []
            for b in range(CAP):
                q, unit = code(value[h * half : (h + 1) * half, b * TILE : (b + 1) * TILE])
                q1s[h, d, e, b] = q
                units.append(jnp.where(rows4 == places[b], unit, 0.0))
            u1s[h, d, e] = jnp.concatenate(units, axis=0)

            @pl.when(d != 0)
            def _():
                for copy in first_leg(h, d, e):
                    copy.start()

        return carry

    lax.fori_loop(0, len(ORDER), one_owner, 0)

    def second_leg(h, e):
        device = at_z[e] if h == 0 else at_x[e]
        return [
            pltpu.make_async_remote_copy(
                src_ref=s.at[h, e], dst_ref=r.at[h, e], send_sem=ss.at[h, e],
                recv_sem=rs.at[h, e], device_id=device, device_id_type=MESH,
            )
            for s, r, ss, rs in ((q2s, q2r, q2_send, q2_recv), (u2s, u2r, u2_send, u2_recv))
        ]

    step = 64

    def add_up(h, e, into):
        for d in range(1, 4):
            for copy in first_leg(h, d, e):
                copy.wait_recv()

        def some_rows(n, carry):
            span = pl.ds(pl.multiple_of(n * step, step), step)
            sums = [jnp.zeros((step, TILE), jnp.float32) for _ in range(4)]
            for d in range(4):
                q_ref, u_ref = (q1s, u1s) if d == 0 else (q1r, u1r)
                for b in range(CAP):
                    v = q_ref[h, d, e, b, span].astype(jnp.int32).astype(jnp.float32)
                    for j in range(4):
                        row = b * 4 + j
                        sums[j] = sums[j] + v * u_ref[h, d, e, row : row + 1]
            for j in range(4):
                into[j, span] = sums[j]
            return carry

        lax.fori_loop(0, half // step, some_rows, 0)

    for e in (2, 1, 3):
        for h in range(2):
            add_up(h, e, total)
            units = []
            for j in range(4):
                q, unit = code(total[j])
                q2s[h, e, j] = q
                units.append(unit)
            u2s[h, e] = jnp.concatenate(units + units, axis=0)
            for copy in second_leg(h, e):
                copy.start()
    for h in range(2):
        add_up(h, 0, own.at[h])
    for h in range(2):
        for e in (2, 1, 3):
            for copy in second_leg(h, e):
                copy.wait_recv()

    for h in range(2):

        def finish(n, carry):
            span = pl.ds(pl.multiple_of(n * step, step), step)
            rows = pl.ds(pl.multiple_of(h * half + n * step, step), step)
            for j in range(4):
                v = own[h, j, span]
                for e in (1, 2, 3):
                    v = v + q2r[h, e, j, span].astype(jnp.int32).astype(jnp.float32) * u2r[h, e, j : j + 1]
                out[rows, j * TILE : (j + 1) * TILE] = v
            return carry

        lax.fori_loop(0, half // step, finish, 0)

    for copy in first_up + first_down + to_mate + list(passed.values()) + list(relayed.values()):
        copy.wait_send()
    for h in range(2):
        for e in range(4):
            for d in range(1, 4):
                for copy in first_leg(h, d, e):
                    copy.wait_send()
            if e:
                for copy in second_leg(h, e):
                    copy.wait_send()


def ladder(table, chosen, amplitudes, tiles):
    rows = amplitudes.shape[0]
    half, every = rows // 2, tiles.shape[0] * 8
    vm, dma = pltpu.VMEM, pltpu.SemaphoreType.DMA
    first_q, first_u = (2, 4, 4, CAP, half, TILE), (2, 4, 4, 8, TILE)
    second_q, second_u = (2, 4, 4, half, TILE), (2, 4, 8, TILE)
    return pl.pallas_call(
        kernel,
        out_shape=jax.ShapeDtypeStruct((rows, 4 * TILE), jnp.float32),
        in_specs=[pl.BlockSpec(memory_space=pltpu.SMEM)] * 2 + [pl.BlockSpec(memory_space=pl.ANY)] * 2,
        out_specs=pl.BlockSpec(memory_space=pltpu.VMEM),
        scratch_shapes=[
            vm(amplitudes.shape, jnp.bfloat16),
            vm((every + 1, TILE, TILE), jnp.bfloat16),
            vm(first_q, jnp.int16), vm(first_u, jnp.float32), vm(first_q, jnp.int16), vm(first_u, jnp.float32),
            vm(second_q, jnp.int16), vm(second_u, jnp.float32), vm(second_q, jnp.int16), vm(second_u, jnp.float32),
            vm((2, 4, half, TILE), jnp.float32), vm((4, half, TILE), jnp.float32),
            dma, dma((PIECES,)), dma((7, PIECES)), dma((7, PIECES)),
            dma((2, 4, 4)), dma((2, 4, 4)), dma((2, 4, 4)), dma((2, 4, 4)),
            dma((2, 4)), dma((2, 4)), dma((2, 4)), dma((2, 4)),
        ],
        compiler_params=pltpu.CompilerParams(
            collective_id=0, has_side_effects=True, vmem_limit_bytes=56 * 2**20
        ),
    )(table, chosen, amplitudes, tiles)


def shards(
    amplitudes, integral_tiles, tile_cd, tile_ab, slot_tile, residual_in, occ_level, vir_level
):
    mine = lax.axis_index("vir")
    kinds = amplitudes.shape[1] // TILE
    count = tile_cd.shape[1]
    my_kinds = lax.dynamic_index_in_dim(tile_cd, mine, 0, keepdims=False)
    my_tiles = lax.dynamic_index_in_dim(tile_ab, mine, 0, keepdims=False)
    match = slot_tile[:, None] == my_tiles[None, :]
    number = jnp.arange(1, count + 1, dtype=jnp.float32)[:, None]
    of_kind = jnp.where(my_kinds[:, None] == jnp.arange(kinds, dtype=jnp.int32), number, 0.0)
    named = jnp.dot(match.astype(jnp.float32), of_kind, precision=lax.Precision.HIGHEST).astype(jnp.int32)
    table = jnp.where(named == 0, count, named - 1).reshape(-1)
    r = jnp.any(match, axis=1).reshape(-1, 4)
    least = jnp.where(r[:, 0], 0, jnp.where(r[:, 1], 1, 2))
    most = jnp.where(r[:, 3], 3, jnp.where(r[:, 2], 2, 1))
    chosen = jnp.stack([least, most], axis=1).astype(jnp.int32).reshape(-1)
    by_slot = ladder(table, chosen, amplitudes, integral_tiles[0])
    return (residual_in + by_slot) / (occ_level[:, None] - vir_level[None, :])


def solution(mesh):
    in_specs = (
        P("occ", "vir"),
        P("vir", "occ", None, None),
        P(),
        P(),
        P(),
        P("occ", "vir"),
        P("occ"),
        P("vir"),
    )
    out_specs = P("occ", "vir")
    return jax.shard_map(shards, mesh=mesh, in_specs=in_specs, out_specs=out_specs, check_vma=False)
```

time: 297 us -> 94.4 us (0.32)
  waiting for transfers between devices: 160 us -> 0 us
  Pallas kernels: 0 us -> 87.3 us
  local copies, waits for them, and re-layouts: 87.7 us -> 2.37 us
  matrix products: 29.5 us -> 1.02 us
  between operations: 13.5 us -> 0.06 us
    reduce_scatter x1 -> x0, waiting for transfers between devices: 108 us -> none  [shards(): summed = lax.psum_scatter(spread, 'vir', scatter_dimension=1, tiled=True)]
    pallas_call x0 -> x1, Pallas kernels: none -> 87.3 us  [ladder(): pl.pallas_call(kernel, out_shape=jax.ShapeDtypeStruct((rows, 4 * TILE), j...]
    all_gather x1 -> x0, waiting for transfers between devices: 51 us -> none  [shards(): lax.all_gather(integral_tiles, 'occ', axis=1, tiled=True)[0]]
    scatter x1 -> x0, local copies, waits for them, and re-layouts: 39.9 us -> none  [shards(): empty.at[column_of, my_kinds]]
    dot_general x2 -> x1, matrix products: 29.5 us -> 1.02 us  [shards(): jnp.dot(match.astype(jnp.float32), of_kind, precision=lax.Precision.HIGHEST)]
    transpose x1 -> x0, local copies, waits for them, and re-layouts: 19.5 us -> none  [shards(): jnp.einsum('rcs,cq->rqs', partial_value, placing, precision=lax.Precision...]
    dot_general x1 -> x0, local copies, waits for them, and re-layouts: 10.3 us -> none  [shards(): jnp.einsum('rkt,ckts->rcs', left, weight, preferred_element_type=jnp.floa...]
    broadcast_in_dim x1 -> x0, local copies, waits for them, and re-layouts: 8.84 us -> none  [shards(): empty = jnp.zeros((groups * CAP, kind_count, tile, tile), jnp.bfloat16)]
  transfers between devices with their start and end apart: 2 -> 0, of which waited for: 2 -> 0; matrix products, arithmetic and copies ran while one was open for 2% -> 0% of each run, Pallas kernels for 0% -> 0%
where the time goes in v1:
time: 94.4 us; the launch traced here: 94.2 us
  Pallas kernels  87.3 us (92%)
  other arithmetic  3.4 us (4%)
  local copies, waits for them, and re-layouts  2.37 us (3%)
  matrix products  1.02 us (1%)
    pallas_call x1, Pallas kernels, ladder(): pl.pallas_call(kernel, out_shape=jax.ShapeDtypeStruct((rows, 4 * TILE), j...  87.3 us
    div x1, other arithmetic, shards(): return (residual_in + by_slot) / (occ_level[:, None] - vir_level[None, :])  2.41 us

profile of v1, /device:TPU:1, one launch (start us, length us, event | category | flops | bytes accessed | tf_op | source)
XLA Modules:
  0.0 94.2 jit_solution(5120164653236598092)
XLA Ops:
  0.0 0.0 copy-start.1
  0.0 0.0 copy-start.2
  0.0 0.0 copy-start
  0.0 0.8 constant_dynamic-slice_fusion
  0.8 0.8 compare_reduce_fusion
  1.7 0.1 reshape.19
  1.8 1.0 %add_select_fusion = s32[64,24]{0,1:T(8,128)S(1)} fusion(f32[256]{0:T(256)S(1)} %iota_add_fusion, s32[256]{0:T(256)S(1)} %bitcast.6, s32[256]{0:T(256)S(1)} %bitcast.5, s32[64]{0:T(128)} %param.12), kind=kOutput, calls=%fused_computation.11 | convolution fusion | flops 4753408 | bytes 9472 | tf_op jit(solution)/shard_map/dot_general | solution.py:276
  2.8 0.1 select_select_fusion.1
  2.9 0.1 pad_add_fusion
  3.0 0.7 reshape.20.chosen
  3.6 0.1 copy.14
  3.7 0.7 reshape.18.table
  4.4 87.3 %shard_map.82 = f32[512,512]{1,0:T(8,128)} custom-call(s32[1536]{0:T(1024)} %reshape.18.table, s32[32]{0:T(128)} %reshape.20.chosen, bf16[512,3072]{1,0:T(8,128)(2,1)} %amp_hbm.1, bf16[32,128,128]{2,1,0:T(8,128)(2,1)} %bitcast.3), custom_call_target="tpu_custom_call" | custom-call | tf_op jit(solution)/shard_map/pallas_call | solution.py:244
  91.7 0.0 copy-done.1
  91.7 0.0 copy-done.2
  91.7 0.0 copy-done
  91.8 2.4 %subtract_divide_fusion = f32[512,512]{1,0:T(8,128)} fusion(f32[512,512]{1,0:T(8,128)S(1)} %copy-done, f32[512,512]{1,0:T(8,128)} %shard_map.82, f32[512]{0:T(512)S(1)} %copy-done.1, f32[512]{0:T(512)S(1)} %copy-done.2), kind=kLoop, calls=%fused_computation.1 | loop fusion | flops 786432 | bytes 3149824 | tf_op jit(solution)/shard_map/div | solution.py:283
  (1 shorter events, 0.0 us)
Async XLA Ops:
  0.0 91.7 %copy-start.1 = (f32[512]{0:T(512)S(1)}, f32[512]{0:T(512)}, u32[]{:S(2)}) copy-start(f32[512]{0:T(512)} %param.15) | copy-start | bytes 6148
  0.0 91.7 %copy-start.2 = (f32[512]{0:T(512)S(1)}, f32[512]{0:T(512)}, u32[]{:S(2)}) copy-start(f32[512]{0:T(512)} %param.14) | copy-start | bytes 6148
  0.0 91.7 %copy-start = (f32[512,512]{1,0:T(8,128)S(1)}, f32[512,512]{1,0:T(8,128)}, u32[]{:S(2)}) copy-start(f32[512,512]{1,0:T(8,128)} %param.13) | copy-start | bytes 3145732

commit v2 on v1

--- a/solution.py
+++ b/solution.py
@@ -1,3 +1,5 @@
+import functools
+
 import jax
 import jax.numpy as jnp
 from jax import lax
@@ -8,13 +10,16 @@
 CAP = 2
 TILE = 128
 MESH = pl.DeviceIdType.MESH
-PIECES = 4
+PIECES = 8
+AHEAD = 2
 FULL = 32767.0
 
 ORDER = (
     (2, 2), (2, 1), (1, 2), (2, 3), (3, 2), (2, 0), (0, 2), (1, 1),
     (3, 3), (1, 3), (3, 1), (1, 0), (3, 0), (0, 1), (0, 3), (0, 0),
 )
+EARLY = (3, 4, 4, 5, 6, 6, 7, 7, 8, 8, 8, 8, 8, 8, 8, 8)
+LATE = (8,) * 16
 
 
 def pick(i, values):
@@ -30,9 +35,9 @@
 
 
 def kernel(
-    table, chosen, amp_hbm, tiles_hbm, out,
-    amp, pool, q1s, u1s, q1r, u1r, q2s, u2s, q2r, u2r, own, total,
-    amp_sem, local_sem, gs_send, gs_recv, q1_send, q1_recv, u1_send, u1_recv, q2_send, q2_recv, u2_send, u2_recv,
+    need, table, chosen, sorting, amp_hbm, tiles_ref, out,
+    amp, sorted_tiles, land, pool, q1s, u1s, q1r, u1r, q2s, u2s, q2r, u2r, own, total,
+    amp_sem, gs_send, gs_recv, q1_send, q1_recv, u1_send, u1_recv, q2_send, q2_recv, u2_send, u2_recv,
 ):
     occ, vir = lax.axis_index("occ"), lax.axis_index("vir")
     y, core = occ // 2, occ % 2
@@ -42,7 +47,7 @@
     mate = (y * 2 + 1 - core, vir)
     at_x = [(occ, ((x + d) % 4) * 4 + z) for d in range(4)]
     at_z = [(occ, x * 4 + (z + d) % 4) for d in range(4)]
-    own_tiles = tiles_hbm.shape[0]
+    own_tiles = tiles_ref.shape[0]
     part = own_tiles // PIECES
     kinds = amp_hbm.shape[1] // TILE
     half = amp_hbm.shape[0] // 2
@@ -54,13 +59,13 @@
     greeted = [up, down, mate] + at_x[1:] + at_z[1:]
     for other in greeted:
         pl.semaphore_signal(barrier, inc=1, device_id=other, device_id_type=MESH)
+    for n in range(own_tiles):
+        sorted_tiles[n] = tiles_ref[sorting[n]]
+    pool[pool.shape[0] - 1] = jnp.zeros((TILE, TILE), pool.dtype)
     pl.semaphore_wait(barrier, len(greeted))
 
-    def place(yy, cc, piece):
-        return pool.at[pl.ds(((yy % 4) * 2 + cc) * own_tiles + piece * part, part)]
-
-    def mine(piece):
-        return tiles_hbm.at[pl.ds(piece * part, part)]
+    def place(yy, cc, piece, first=0, size=part):
+        return land[piece].at[pl.ds(((yy % 4) * 2 + cc) * part + first, size)]
 
     def send(kind, piece, source, target, device):
         return pltpu.make_async_remote_copy(
@@ -69,48 +74,54 @@
         )
 
     pieces = range(PIECES)
-    low, high = pieces[: PIECES // 2], pieces[PIECES // 2 :]
+    mid = part // 2
+
+    def mine(p):
+        return sorted_tiles.at[pl.ds(p * part, part)]
+
+    def pass_on(kind, p, yy, first, device):
+        spot = place(yy, core, p, first, mid)
+        return send(kind, p, spot, spot, device)
+
+    def relay(kind, p, yy):
+        return send(kind, p, place(yy, core, p), place(yy, core, p), mate)
+
     first_up = [send(0, p, mine(p), place(y, core, p), up) for p in pieces]
     first_down = [send(1, p, mine(p), place(y, core, p), down) for p in pieces]
-    to_mate = [send(3, p, mine(p), place(y, core, p), mate) for p in pieces]
-    here = [pltpu.make_async_copy(mine(p), place(y, core, p), local_sem.at[p]) for p in pieces]
-    for a, b in zip(pieces, list(high) + list(low)):
-        first_up[a].start()
-        first_down[b].start()
-    for p in pieces:
+    on_up = [pass_on(2, p, y + 3, 0, up) for p in pieces]
+    on_down = [pass_on(3, p, y + 1, mid, down) for p in pieces]
+    to_mate = [send(4, p, mine(p), place(y, core, p), mate) for p in pieces]
+    low_mate = [relay(5, p, y + 3) for p in pieces]
+    high_mate = [relay(6, p, y + 1) for p in pieces]
+    far_mate = [relay(7, p, y + 2) for p in pieces]
+
+    def own_piece(p):
+        first_up[p].start()
+        first_down[p].start()
         to_mate[p].start()
-        here[p].start()
-    pool[pool.shape[0] - 1] = jnp.zeros((TILE, TILE), pool.dtype)
-    passed, relayed = {}, {}
-
-    def relay(kind, p, yy):
-        relayed[kind, p] = send(kind, p, place(yy, core, p), place(yy, core, p), mate)
-        relayed[kind, p].start()
-
-    for a, b in zip(pieces, list(high) + list(low)):
-        first_up[a].wait_recv()
-        if a in low:
-            passed[a] = send(2, a, place(y + 3, core, a), place(y + 3, core, a), up)
-            passed[a].start()
-        first_down[b].wait_recv()
-        if b in high:
-            passed[b] = send(2, b, place(y + 1, core, b), place(y + 1, core, b), down)
-            passed[b].start()
-        relay(4, a, y + 3)
-        relay(5, b, y + 1)
-    for a, b in zip(low, high):
-        for p in (a, b):
-            passed[p].wait_recv()
-            relay(6, p, y + 2)
-    load_amp.wait()
-    for p in pieces:
-        here[p].wait()
-        to_mate[p].wait_recv()
-        relayed[4, p].wait_recv()
-        relayed[5, p].wait_recv()
-    for a, b in zip(low, high):
-        relayed[6, a].wait_recv()
-        relayed[6, b].wait_recv()
+
+    def arrive(p):
+        first_up[p].wait_recv()
+        on_up[p].start()
+        low_mate[p].start()
+        first_down[p].wait_recv()
+        on_down[p].start()
+        high_mate[p].start()
+        if p + AHEAD < PIECES:
+            own_piece(p + AHEAD)
+
+    def arrive_far(p):
+        on_up[p].wait_recv()
+        on_down[p].wait_recv()
+        far_mate[p].start()
+
+    def complete(p):
+        for copies in (to_mate, low_mate, high_mate, far_mate):
+            copies[p].wait_recv()
+        base = p * part * 8
+        for n in range(8):
+            pool[pl.ds(base + n * part, part)] = land[p][pl.ds(n * part, part)]
+        pool[pl.ds(base + occ * part, part)] = sorted_tiles[pl.ds(p * part, part)]
 
     def first_leg(h, d, e):
         device = (occ, ((x + d) % 4) * 4 + z) if h == 0 else (occ, x * 4 + (z + d) % 4)
@@ -156,7 +167,10 @@
 
         return carry
 
-    lax.fori_loop(0, len(ORDER), one_owner, 0)
+    def owners(available):
+        ready = [i for i, n in enumerate(need) if n == available]
+        if ready:
+            lax.fori_loop(ready[0], ready[-1] + 1, one_owner, 0)
 
     def second_leg(h, e):
         device = at_z[e] if h == 0 else at_x[e]
@@ -191,7 +205,7 @@
 
         lax.fori_loop(0, half // step, some_rows, 0)
 
-    for e in (2, 1, 3):
+    def second(e):
         for h in range(2):
             add_up(h, e, total)
             units = []
@@ -202,6 +216,26 @@
             u2s[h, e] = jnp.concatenate(units + units, axis=0)
             for copy in second_leg(h, e):
                 copy.start()
+
+    for p in range(AHEAD):
+        own_piece(p)
+    for p in pieces:
+        arrive(p)
+        if p == 0:
+            load_amp.wait()
+        else:
+            arrive_far(p - 1)
+            complete(p - 1)
+            owners(p)
+    arrive_far(PIECES - 1)
+    if need[6] < PIECES:
+        second(2)
+    complete(PIECES - 1)
+    owners(PIECES)
+    if need[6] == PIECES:
+        second(2)
+    second(1)
+    second(3)
     for h in range(2):
         add_up(h, 0, own.at[h])
     for h in range(2):
@@ -223,8 +257,9 @@
 
         lax.fori_loop(0, half // step, finish, 0)
 
-    for copy in first_up + first_down + to_mate + list(passed.values()) + list(relayed.values()):
-        copy.wait_send()
+    for copies in (first_up, first_down, on_up, on_down, to_mate, low_mate, high_mate, far_mate):
+        for copy in copies:
+            copy.wait_send()
     for h in range(2):
         for e in range(4):
             for d in range(1, 4):
@@ -235,31 +270,38 @@
                     copy.wait_send()
 
 
-def ladder(table, chosen, amplitudes, tiles):
+def ladder(need, barrier_id, table, chosen, sorting, amplitudes, tiles):
     rows = amplitudes.shape[0]
     half, every = rows // 2, tiles.shape[0] * 8
     vm, dma = pltpu.VMEM, pltpu.SemaphoreType.DMA
     first_q, first_u = (2, 4, 4, CAP, half, TILE), (2, 4, 4, 8, TILE)
     second_q, second_u = (2, 4, 4, half, TILE), (2, 4, 8, TILE)
     return pl.pallas_call(
-        kernel,
+        functools.partial(kernel, need),
         out_shape=jax.ShapeDtypeStruct((rows, 4 * TILE), jnp.float32),
-        in_specs=[pl.BlockSpec(memory_space=pltpu.SMEM)] * 2 + [pl.BlockSpec(memory_space=pl.ANY)] * 2,
+        in_specs=[pl.BlockSpec(memory_space=pltpu.SMEM)] * 3
+        + [pl.BlockSpec(memory_space=pl.ANY), pl.BlockSpec(memory_space=pltpu.VMEM)],
         out_specs=pl.BlockSpec(memory_space=pltpu.VMEM),
         scratch_shapes=[
             vm(amplitudes.shape, jnp.bfloat16),
+            vm(tiles.shape, jnp.bfloat16),
+            [vm((every // PIECES, TILE, TILE), jnp.bfloat16) for _ in range(PIECES)],
             vm((every + 1, TILE, TILE), jnp.bfloat16),
             vm(first_q, jnp.int16), vm(first_u, jnp.float32), vm(first_q, jnp.int16), vm(first_u, jnp.float32),
             vm(second_q, jnp.int16), vm(second_u, jnp.float32), vm(second_q, jnp.int16), vm(second_u, jnp.float32),
             vm((2, 4, half, TILE), jnp.float32), vm((4, half, TILE), jnp.float32),
-            dma, dma((PIECES,)), dma((7, PIECES)), dma((7, PIECES)),
+            dma, dma((8, PIECES)), dma((8, PIECES)),
             dma((2, 4, 4)), dma((2, 4, 4)), dma((2, 4, 4)), dma((2, 4, 4)),
             dma((2, 4)), dma((2, 4)), dma((2, 4)), dma((2, 4)),
         ],
         compiler_params=pltpu.CompilerParams(
-            collective_id=0, has_side_effects=True, vmem_limit_bytes=56 * 2**20
+            collective_id=barrier_id, has_side_effects=True, vmem_limit_bytes=60 * 2**20
         ),
-    )(table, chosen, amplitudes, tiles)
+    )(table, chosen, sorting, amplitudes, tiles)
+
+
+def choose(value, cases):
+    return sum(jnp.where(value == case, result, 0) for case, result in cases)
 
 
 def shards(
@@ -267,11 +309,32 @@
 ):
     mine = lax.axis_index("vir")
     kinds = amplitudes.shape[1] // TILE
-    count = tile_cd.shape[1]
+    groups, count = tile_cd.shape
+    holders = lax.axis_size("occ")
+    part = count // holders // PIECES
+
+    hit = tile_ab[:, :, None] == slot_tile
+    slot = jnp.sum(jnp.where(hit, lax.broadcasted_iota(jnp.int32, hit.shape, 2), 0), axis=2)
+    group = lax.broadcasted_iota(jnp.int32, slot.shape, 0)
+    ox, oz = slot // 16, slot // 4 % 4
+    steps = (ox - group // 4 + 4) % 4 * 4 + (oz - group % 4 + 4) % 4
+    turn = choose(steps, [(o[0] * 4 + o[1], n) for n, o in enumerate(ORDER)])
+    key = (turn * count + lax.broadcasted_iota(jnp.int32, slot.shape, 1)).reshape(groups, holders, -1)
+    place = jnp.sum((key[:, :, None, :] < key[:, :, :, None]).astype(jnp.int32), axis=3)
+    allowed = choose(turn, [(n, p * part) for n, p in enumerate(EARLY)]).reshape(place.shape)
+    crowded = jnp.any(place >= allowed)
+
+    my_place = lax.dynamic_index_in_dim(place, mine, 0, keepdims=False)
+    holder = lax.broadcasted_iota(jnp.int32, my_place.shape, 0)
+    at = (my_place // part * (holders * part) + holder * part + my_place % part).reshape(-1)
+    held = lax.dynamic_index_in_dim(my_place, lax.axis_index("occ"), 0, keepdims=False)
+    ordinal = jnp.arange(held.shape[0], dtype=jnp.int32)
+    sorting = jnp.sum(jnp.where(held[None, :] == ordinal[:, None], ordinal[None, :], 0), axis=1)
+
     my_kinds = lax.dynamic_index_in_dim(tile_cd, mine, 0, keepdims=False)
     my_tiles = lax.dynamic_index_in_dim(tile_ab, mine, 0, keepdims=False)
     match = slot_tile[:, None] == my_tiles[None, :]
-    number = jnp.arange(1, count + 1, dtype=jnp.float32)[:, None]
+    number = (at + 1).astype(jnp.float32)[:, None]
     of_kind = jnp.where(my_kinds[:, None] == jnp.arange(kinds, dtype=jnp.int32), number, 0.0)
     named = jnp.dot(match.astype(jnp.float32), of_kind, precision=lax.Precision.HIGHEST).astype(jnp.int32)
     table = jnp.where(named == 0, count, named - 1).reshape(-1)
@@ -279,8 +342,18 @@
     least = jnp.where(r[:, 0], 0, jnp.where(r[:, 1], 1, 2))
     most = jnp.where(r[:, 3], 3, jnp.where(r[:, 2], 2, 1))
     chosen = jnp.stack([least, most], axis=1).astype(jnp.int32).reshape(-1)
-    by_slot = ladder(table, chosen, amplitudes, integral_tiles[0])
-    return (residual_in + by_slot) / (occ_level[:, None] - vir_level[None, :])
+
+    tiles = integral_tiles[0]
+    by_slot = ladder(EARLY, 0, table, chosen, sorting, amplitudes, tiles)
+
+    def update(value):
+        return (residual_in + value) / (occ_level[:, None] - vir_level[None, :])
+
+    return lax.cond(
+        crowded,
+        lambda: update(ladder(LATE, 1, table, chosen, sorting, amplitudes, tiles)),
+        lambda: update(by_slot),
+    )
 
 
 def solution(mesh):

time: 94.4 us -> 88.3 us (0.935)
  Pallas kernels: 87.3 us -> 75.8 us
  other arithmetic: 3.4 us -> 7.76 us
    pallas_call x1, Pallas kernels: 87.3 us -> 75.8 us  [ladder(): pl.pallas_call(functools.partial(kernel, need), out_shape=jax.ShapeDtypeS...]
    reduce_sum x0 -> x3, other arithmetic: none -> 3.94 us  [the longest x1 2.91 us: shards(): jnp.sum((key[:, :, None, :] < key[:, :, :, None]).astype(jnp.int32), axis=3)]
    unnamed x6 -> x8, local copies, waits for them, and re-layouts: 0.01 us -> 0.98 us
    div x1 -> x2, other arithmetic: 2.41 us -> 1.75 us  [the longest x1 1.75 us: update(): return (residual_in + value) / (occ_level[:, None] - vir_level[None, :])]
where the time goes in v2:
time: 88.3 us; the launch traced here: 88 us
  Pallas kernels  75.8 us (86%)
  other arithmetic  7.76 us (9%)
  local copies, waits for them, and re-layouts  2.4 us (3%)
  matrix products  1.01 us (1%)
    pallas_call x1, Pallas kernels, ladder(): pl.pallas_call(functools.partial(kernel, need), out_shape=jax.ShapeDtypeS...  75.8 us
    reduce_sum x1, other arithmetic, shards(): jnp.sum((key[:, :, None, :] < key[:, :, :, None]).astype(jnp.int32), axis=3)  2.91 us

profile of v2, /device:TPU:1, one launch (start us, length us, event | category | flops | bytes accessed | tf_op | source)
XLA Modules:
  0.0 88.0 jit_solution(13139565513129070959)
XLA Ops:
  0.0 0.7 constant_dynamic-slice_fusion.2
  0.8 0.8 compare_reduce_fusion
  1.6 0.1 reshape.511
  1.7 0.1 iota.83
  1.8 0.1 iota.84
  1.9 0.1 select_select_fusion.1
  1.9 0.1 pad_add_fusion
  2.0 0.1 reshape.512.chosen
  2.1 0.9 %select_reduce_fusion = s32[16,256]{1,0:T(8,128)S(1)} fusion(s32[16,256]{1,0:T(8,128)} %param.13, s32[64]{0:T(128)} %param.14), kind=kLoop, calls=%fused_computation.4 | loop fusion | flops 782336 | bytes 33024 | tf_op jit(solution)/shard_map/reduce_sum | solution.py:317
  3.0 0.1 reduce_sum.30
  3.1 0.3 multiply_add_fusion
  3.4 2.9 %convert_reduce_fusion = s32[16,8,32]{2,1,0:T(8,128)S(1)} fusion(s32[16,8,32]{2,1,0:T(8,128)S(1)} %get-tuple-element.45), kind=kLoop, calls=%fused_computation.2 | loop fusion | flops 389120 | bytes 32768 | tf_op jit(solution)/shard_map/reduce_sum | solution.py:323
  6.3 0.7 fusion.18
  7.8 0.1 squeeze.16
  7.9 0.1 select_reduce_fusion.1.sorting
  8.0 1.0 %add_select_fusion.5 = s32[64,24]{0,1:T(8,128)S(1)} fusion(f32[256]{0:T(256)S(1)} %add_convert_fusion, s32[256]{0:T(256)S(1)} %bitcast.9, s32[256]{0:T(256)S(1)} %bitcast.8, s32[64]{0:T(128)} %param.14), kind=kOutput, calls=%fused_computation.50 | convolution fusion | flops 4753408 | bytes 9472 | tf_op jit(solution)/shard_map/dot_general | solution.py:339
  9.0 0.1 copy.16
  9.1 0.1 reshape.510.table
  9.2 0.0 copy-start.2
  9.2 0.0 copy-start.3
  9.2 75.8 %shard_map.84 = f32[512,512]{1,0:T(8,128)} custom-call(s32[1536]{0:T(1024)S(1)} %reshape.510.table, s32[32]{0:T(128)S(1)} %reshape.512.chosen, s32[32]{0:T(128)S(1)} %select_reduce_fusion.1.sorting, bf16[512,3072]{1,0:T(8,128)(2,1)} %amp_hbm.1, bf16[32,128,128]{2,1,0:T(8,128)(2,1)} %bitcast.5), custom_call_target="tpu_custom_call" | custom-call | tf_op jit(solution)/shard_map/pallas_call | solution.py:279
  85.0 2.0 %conditional.1 = (f32[512,512]{1,0:T(8,128)S(1)}) conditional(s32[]{:T(128)} %convert_element_type.18, (f32[512,512]{1,0:T(8,128)}, f32[512,512]{1,0:T(8,128)}, f32[512]{0:T(512)S(1)}, f32[512]{0:T(512)S(1)}) %tuple.28, (s32[1536]{0:T(1024)S(1)}, s32[32]{0:T(128)S(1)}, s32[32]{0:T(128)S(1)}, bf16[512,3072]{1,0:T(8,128)(2,1)S(1)}, ...), branch_computations={%region_5.6_spmd, %region_6.7_spmd} | conditional | flops 786432 | bytes 3149832 | solution.py:352
  85.1 1.8 %subtract_divide_fusion = f32[512,512]{1,0:T(8,128)S(1)} fusion(f32[512,512]{1,0:T(8,128)} %get-tuple-element.32, f32[512,512]{1,0:T(8,128)} %get-tuple-element.33, f32[512]{0:T(512)S(1)} %get-tuple-element.35, f32[512]{0:T(512)S(1)} %get-tuple-element.34), kind=kLoop, calls=%fused_computation | loop fusion | flops 786432 | bytes 3149824 | tf_op jit(solution)/shard_map/cond/branch_0_fun/div | solution.py:350
  87.0 1.0 %copy-done.1 = f32[512,512]{1,0:T(8,128)} copy-done((f32[512,512]{1,0:T(8,128)}, f32[512,512]{1,0:T(8,128)S(1)}, u32[]{:S(2)}) %copy-start.1) | copy-done | bytes 1048600
  (13 shorter events, 0.1 us)
Async XLA Ops:
  9.2 75.8 %copy-start = (bf16[512,3072]{1,0:T(8,128)(2,1)S(1)}, bf16[512,3072]{1,0:T(8,128)(2,1)}, u32[]{:S(2)}) copy-start(bf16[512,3072]{1,0:T(8,128)(2,1)} %amp_hbm.1) | copy-start | bytes 9437188
  9.2 75.8 %copy-start.2 = (f32[512]{0:T(512)S(1)}, f32[512]{0:T(512)}, u32[]{:S(2)}) copy-start(f32[512]{0:T(512)} %param.16) | copy-start | bytes 6148
  9.2 75.8 %copy-start.3 = (f32[512]{0:T(512)S(1)}, f32[512]{0:T(512)}, u32[]{:S(2)}) copy-start(f32[512]{0:T(512)} %param.17) | copy-start | bytes 6148
  87.0 1.0 %copy-start.1 = (f32[512,512]{1,0:T(8,128)}, f32[512,512]{1,0:T(8,128)S(1)}, u32[]{:S(2)}) copy-start(f32[512,512]{1,0:T(8,128)S(1)} %get-tuple-element.59) | copy-start | bytes 3145732

commit v3 on v1

v3 whole, which is shorter than its diff:
```python
import functools

import jax
import jax.numpy as jnp
from jax import lax
from jax.experimental import pallas as pl
from jax.experimental.pallas import tpu as pltpu
from jax.sharding import PartitionSpec as P

CAP = 2
TILE = 128
MESH = pl.DeviceIdType.MESH
PIECES = 16
AHEAD = 3
FAR_LAG, LAG = 1, 2
FULL = 32767.0

ORDER = (
    (2, 2), (2, 1), (1, 2), (2, 3), (3, 2), (2, 0), (0, 2), (1, 1),
    (3, 3), (1, 3), (3, 1), (1, 0), (3, 0), (0, 1), (0, 3), (0, 0),
)
EARLY = (5, 7, 8, 10, 11, 12, 13, 14, 15, 15, 16, 16, 16, 16, 16, 16)
LATE = (16,) * 16


def pick(i, values):
    out = jnp.int32(values[0])
    for n, v in enumerate(values[1:], 1):
        out = jnp.where(i == n, jnp.int32(v), out)
    return out


def code(v):
    top = jnp.maximum(jnp.max(jnp.abs(v), axis=0, keepdims=True), 1e-30)
    return jnp.round(v * (FULL / top)).astype(jnp.int32).astype(jnp.int16), top * (1.0 / FULL)


def within(index, size):
    return jnp.minimum(jnp.maximum(index, 0), size - 1)


def cases(value, results):
    out = jnp.zeros_like(value)
    for n, result in enumerate(results):
        out = jnp.where(value == n, result, out)
    return out


def kernel(
    need, slot_tile, tile_ab, tile_cd, amp_hbm, tiles_hbm, out, crowded,
    amp, tiles, sorted_tiles, land, pool, q1s, u1s, q1r, u1r, q2s, u2s, q2r, u2r, own, total,
    slots_v, turns_v, sorting_v, table_v, sorting, table,
    load_sem, gs_send, gs_recv, q1_send, q1_recv, u1_send, u1_recv, q2_send, q2_recv, u2_send, u2_recv,
):
    occ, vir = lax.axis_index("occ"), lax.axis_index("vir")
    y, core = occ // 2, occ % 2
    x, z = vir // 4, vir % 4
    up = (((y + 1) % 4) * 2 + core, vir)
    down = (((y + 3) % 4) * 2 + core, vir)
    mate = (y * 2 + 1 - core, vir)
    at_x = [(occ, ((x + d) % 4) * 4 + z) for d in range(4)]
    at_z = [(occ, x * 4 + (z + d) % 4) for d in range(4)]
    own_tiles = tiles_hbm.shape[0]
    holders = 8
    part = own_tiles // PIECES
    half = amp_hbm.shape[0] // 2
    kinds = amp_hbm.shape[1] // TILE

    load_tiles = pltpu.make_async_copy(tiles_hbm, tiles, load_sem.at[0])
    load_tiles.start()
    load_amp = pltpu.make_async_copy(amp_hbm, amp, load_sem.at[1])
    load_amp.start()

    barrier = pltpu.get_barrier_semaphore()
    greeted = [up, down, mate] + at_x[1:] + at_z[1:]
    for other in greeted:
        pl.semaphore_signal(barrier, inc=1, device_id=other, device_id_type=MESH)

    groups, count = tile_ab.shape
    ab = tile_ab[...]
    slot = jnp.zeros_like(ab)
    for j in range(1, slot_tile.shape[0]):
        slot = jnp.where(ab == slot_tile[j], j, slot)
    group = lax.broadcasted_iota(jnp.int32, ab.shape, 0)
    steps = (slot // 16 - group // 4 + 4) % 4 * 4 + (slot // 4 % 4 - group % 4 + 4) % 4
    turn_of = [ORDER.index((n // 4, n % 4)) for n in range(16)]
    turn = cases(steps, turn_of)
    slots_v[...] = slot
    turns_v[...] = turn

    lane = lax.broadcasted_iota(jnp.int32, (1, count), 1)
    my_slot, my_turn = slots_v[pl.ds(vir, 1)], turns_v[pl.ds(vir, 1)]
    key = ((lane // own_tiles) * 4096 + my_turn * 256 + lane % own_tiles).astype(jnp.float32)
    row = lax.broadcasted_iota(jnp.int32, (count, count), 0)
    column = lax.broadcasted_iota(jnp.int32, (count, count), 1)
    keys = jnp.broadcast_to(key, (count, count))
    key_down = jnp.sum(jnp.where(row == column, keys, 0.0), axis=1, keepdims=True)
    rank = jnp.sum(jnp.where(key_down < keys, 1.0, 0.0), axis=0, keepdims=True).astype(jnp.int32)
    place_row = lax.broadcasted_iota(jnp.int32, (own_tiles, count), 0) + occ * own_tiles
    number = (lane % own_tiles).astype(jnp.float32)
    held = jnp.sum(jnp.where(rank == place_row, number, 0.0), axis=1, keepdims=True)
    sorting_v[...] = jnp.broadcast_to(held, (own_tiles, TILE)).astype(jnp.int32)
    put_sorting = pltpu.make_async_copy(sorting_v, sorting, load_sem.at[2])
    put_sorting.start()
    load_tiles.wait()
    put_sorting.wait()
    for n in range(own_tiles):
        sorted_tiles[n] = tiles[within(sorting[n, 0], own_tiles)]
    pool[pool.shape[0] - 1] = jnp.zeros((TILE, TILE), pool.dtype)
    pl.semaphore_wait(barrier, len(greeted))

    def place(yy, cc, piece, first=0, size=part):
        return land.at[piece, pl.ds(((yy % 4) * 2 + cc) * part + first, size)]

    def send(kind, piece, source, target, device):
        return pltpu.make_async_remote_copy(
            src_ref=source, dst_ref=target, send_sem=gs_send.at[kind, piece],
            recv_sem=gs_recv.at[kind, piece], device_id=device, device_id_type=MESH,
        )

    mid = part // 2

    def mine(p):
        return sorted_tiles.at[pl.ds(p * part, part)]

    def pass_on(kind, p, yy, first, device):
        spot = place(yy, core, p, first, mid)
        return send(kind, p, spot, spot, device)

    def relay(kind, p, yy):
        return send(kind, p, place(yy, core, p), place(yy, core, p), mate)

    def first_up(p):
        return send(0, p, mine(p), place(y, core, p), up)

    def first_down(p):
        return send(1, p, mine(p), place(y, core, p), down)

    def on_up(p):
        return pass_on(2, p, y + 3, 0, up)

    def on_down(p):
        return pass_on(3, p, y + 1, mid, down)

    def to_mate(p):
        return send(4, p, mine(p), place(y, core, p), mate)

    def low_mate(p):
        return relay(5, p, y + 3)

    def high_mate(p):
        return relay(6, p, y + 1)

    def far_mate(p):
        return relay(7, p, y + 2)

    def own_piece(p):
        first_up(p).start()
        first_down(p).start()
        to_mate(p).start()

    def arrive(p):
        first_up(p).wait_recv()
        on_up(p).start()
        low_mate(p).start()
        first_down(p).wait_recv()
        on_down(p).start()
        high_mate(p).start()

        @pl.when(p + AHEAD < PIECES)
        def _():
            own_piece(p + AHEAD)

    def arrive_far(p):
        on_up(p).wait_recv()
        on_down(p).wait_recv()
        far_mate(p).start()

    def complete(p):
        for copies in (to_mate, low_mate, high_mate, far_mate):
            copies(p).wait_recv()
        base = p * part * holders
        pool[pl.ds(base, part * holders)] = land[p]
        pool[pl.ds(base + occ * part, part)] = sorted_tiles[pl.ds(p * part, part)]

    for p in range(AHEAD):
        own_piece(p)

    table_slots = slot_tile.shape[0]
    slot_row = lax.broadcasted_iota(jnp.int32, (table_slots, count), 0)
    match = jnp.where(slot_row == my_slot, 1.0, 0.0).astype(jnp.bfloat16)
    pos = rank % own_tiles
    at = pos // part * (holders * part) + lane // own_tiles * part + pos % part
    kind_row = lax.broadcasted_iota(jnp.int32, (TILE, count), 0)
    of_kind = jnp.where(kind_row == tile_cd[pl.ds(vir, 1)], (at + 1).astype(jnp.float32), 0.0)
    named = lax.dot_general(
        match, of_kind.astype(jnp.bfloat16), (((1,), (1,)), ((), ())), preferred_element_type=jnp.float32
    ).astype(jnp.int32)
    table_v[0:table_slots] = jnp.where(named == 0, count, named - 1)
    reached = jnp.dot(match, jnp.ones((count, TILE), jnp.bfloat16), preferred_element_type=jnp.float32)
    reached = jnp.minimum(reached, 1.0)
    r = lax.broadcasted_iota(jnp.int32, (table_slots, table_slots), 0)
    c = lax.broadcasted_iota(jnp.int32, (table_slots, table_slots), 1)
    before = jnp.where((r // 4 == c // 4) & (c < r), 1.0, 0.0).astype(jnp.bfloat16)
    rank_in = jnp.dot(before, reached.astype(jnp.bfloat16), preferred_element_type=jnp.float32)
    r = lax.broadcasted_iota(jnp.int32, (table_slots, TILE), 0)
    c = lax.broadcasted_iota(jnp.int32, (table_slots, TILE), 1)
    hit = (reached > 0.0) & (r // 4 * CAP + rank_in.astype(jnp.int32) == c)
    chosen = jnp.sum(jnp.where(hit, r.astype(jnp.float32), 0.0), axis=0, keepdims=True)
    table_v[table_slots : table_slots + 8] = jnp.broadcast_to(chosen, (8, TILE)).astype(jnp.int32)
    put_table = pltpu.make_async_copy(table_v, table, load_sem.at[2])
    put_table.start()

    a = lax.broadcasted_iota(jnp.int32, (count, TILE), 0)
    c = lax.broadcasted_iota(jnp.int32, (count, TILE), 1)
    holds = jnp.where(a // own_tiles == c, 1.0, 0.0).astype(jnp.bfloat16)
    turn = turns_v[...]
    worst = jnp.zeros((groups, TILE), jnp.float32)
    for n, pieces in enumerate(need):
        if pieces < PIECES:
            early = jnp.where(turn <= n, 1.0, 0.0).astype(jnp.bfloat16)
            tally = jnp.dot(early, holds, preferred_element_type=jnp.float32)
            worst = jnp.maximum(worst, tally - pieces * part)
    worst = jnp.max(jnp.max(worst, axis=1, keepdims=True), axis=0, keepdims=True)
    crowded[...] = jnp.broadcast_to(worst, crowded.shape)
    put_table.wait()
    load_amp.wait()

    def first_leg(h, d, e):
        device = (occ, ((x + d) % 4) * 4 + z) if h == 0 else (occ, x * 4 + (z + d) % 4)
        return [
            pltpu.make_async_remote_copy(
                src_ref=s.at[h, d, e], dst_ref=r.at[h, d, e], send_sem=ss.at[h, d, e],
                recv_sem=rs.at[h, d, e], device_id=device, device_id_type=MESH,
            )
            for s, r, ss, rs in ((q1s, q1r, q1_send, q1_recv), (u1s, u1r, u1_send, u1_recv))
        ]

    rows4 = lax.broadcasted_iota(jnp.int32, (4, TILE), 0)

    def one_owner(i, carry):
        dx, dz = pick(i, [o[0] for o in ORDER]), pick(i, [o[1] for o in ORDER])
        owner = ((x + dx) % 4) * 4 + (z + dz) % 4
        slots = [within(table[table_slots, owner * CAP + b], table_slots) for b in range(CAP)]
        value = jnp.zeros((2 * half, CAP * TILE), jnp.float32)
        for k in range(0, kinds, 2):
            rhs = jnp.concatenate(
                [
                    jnp.concatenate([pool[within(table[slots[b], kk], count + 1)] for b in range(CAP)], axis=1)
                    for kk in (k, k + 1)
                ],
                axis=0,
            )
            value = value + jnp.dot(
                amp[:, k * TILE : (k + 2) * TILE], rhs, preferred_element_type=jnp.float32
            )
        for h, d, e in ((0, dx, dz), (1, dz, dx)):
            units = []
            for b in range(CAP):
                q, unit = code(value[h * half : (h + 1) * half, b * TILE : (b + 1) * TILE])
                q1s[h, d, e, b] = q
                units.append(jnp.where(rows4 == slots[b] - owner * 4, unit, 0.0))
            u1s[h, d, e] = jnp.concatenate(units, axis=0)

            @pl.when(d != 0)
            def _():
                for copy in first_leg(h, d, e):
                    copy.start()

        return carry

    def second_leg(h, e):
        near = at_z if h == 0 else at_x
        pairs = ((e, 0, 4),) if e != 2 else ((1, 0, 2), (3, 2, 2))
        return [
            pltpu.make_async_remote_copy(
                src_ref=s.at[h, e, pl.ds(first, size)] if s is q2s else s.at[h, e],
                dst_ref=r.at[h, e, pl.ds(first, size)] if r is q2r else r.at[h, e if e != 2 else e - 2 + first],
                send_sem=ss.at[h, e if to == e else first], recv_sem=rs.at[h, e if to == e else first],
                device_id=near[to], device_id_type=MESH,
            )
            for to, first, size in pairs
            for s, r, ss, rs in ((q2s, q2r, q2_send, q2_recv), (u2s, u2r, u2_send, u2_recv))
        ]

    step = 64

    def add_up(h, e, into):
        for d in range(1, 4):
            for copy in first_leg(h, d, e):
                copy.wait_recv()

        def some_rows(n, carry):
            span = pl.ds(pl.multiple_of(n * step, step), step)
            sums = [jnp.zeros((step, TILE), jnp.float32) for _ in range(4)]
            for d in range(4):
                q_ref, u_ref = (q1s, u1s) if d == 0 else (q1r, u1r)
                for b in range(CAP):
                    v = q_ref[h, d, e, b, span].astype(jnp.int32).astype(jnp.float32)
                    for j in range(4):
                        row = b * 4 + j
                        sums[j] = sums[j] + v * u_ref[h, d, e, row : row + 1]
            for j in range(4):
                into[j, span] = sums[j]
            return carry

        lax.fori_loop(0, half // step, some_rows, 0)

    def second(e):
        for h in range(2):
            add_up(h, e, total)
            if e != 2:
                first = 0 if e == 1 else 2
                for copy in second_leg(h, 2)[first : first + 2]:
                    copy.wait_recv()
                for j in (first, first + 1):
                    passing = q2r[h, 2, j].astype(jnp.int32).astype(jnp.float32)
                    total[j] = total[j] + passing * u2r[h, first, j : j + 1]
            units = []
            for j in range(4):
                q, unit = code(total[j])
                q2s[h, e, j] = q
                units.append(unit)
            u2s[h, e] = jnp.concatenate(units + units, axis=0)
            for copy in second_leg(h, e):
                copy.start()

    early_second = need[6] + LAG + 1 if need[6] < PIECES else None

    def one_piece(p, done):
        @pl.when(p < PIECES)
        def _():
            arrive(p)

        if early_second is not None:

            @pl.when(p == early_second)
            def _():
                second(2)

        @pl.when(p >= LAG)
        def _():
            complete(p - LAG)

        ready = jnp.int32(0)
        for n in need:
            ready = ready + jnp.where(p >= n + LAG - 1, 1, 0)
        lax.fori_loop(done, ready, one_owner, 0)
        @pl.when((p >= FAR_LAG) & (p < PIECES + FAR_LAG))
        def _():
            arrive_far(p - FAR_LAG)

        return ready

    lax.fori_loop(0, PIECES + LAG, one_piece, jnp.int32(0))
    if early_second is None:
        second(2)
    second(1)
    second(3)
    for h in range(2):
        add_up(h, 0, own.at[h])
    for h in range(2):
        for e in (1, 3):
            for copy in second_leg(h, e):
                copy.wait_recv()

    for h in range(2):

        def finish(n, carry):
            span = pl.ds(pl.multiple_of(n * step, step), step)
            rows = pl.ds(pl.multiple_of(h * half + n * step, step), step)
            for j in range(4):
                v = own[h, j, span]
                for e in (1, 3):
                    v = v + q2r[h, e, j, span].astype(jnp.int32).astype(jnp.float32) * u2r[h, e, j : j + 1]
                out[rows, j * TILE : (j + 1) * TILE] = v
            return carry

        lax.fori_loop(0, half // step, finish, 0)

    def all_sent(p, carry):
        for copies in (first_up, first_down, on_up, on_down, to_mate, low_mate, high_mate, far_mate):
            copies(p).wait_send()
        return carry

    lax.fori_loop(0, PIECES, all_sent, 0)
    for h in range(2):
        for e in range(4):
            for d in range(1, 4):
                for copy in first_leg(h, d, e):
                    copy.wait_send()
            if e:
                for copy in second_leg(h, e):
                    copy.wait_send()


def ladder(need, barrier_id, slot_tile, tile_ab, tile_cd, amplitudes, tiles):
    rows = amplitudes.shape[0]
    half, every = rows // 2, tiles.shape[0] * 8
    vm, dma = pltpu.VMEM, pltpu.SemaphoreType.DMA
    first_q, first_u = (2, 4, 4, CAP, half, TILE), (2, 4, 4, 8, TILE)
    second_q, second_u = (2, 4, 4, half, TILE), (2, 4, 8, TILE)
    rows_of_table = slot_tile.shape[0] + 8
    return pl.pallas_call(
        functools.partial(kernel, need),
        out_shape=(
            jax.ShapeDtypeStruct((rows, 4 * TILE), jnp.float32),
            jax.ShapeDtypeStruct((8, TILE), jnp.float32),
        ),
        in_specs=[
            pl.BlockSpec(memory_space=pltpu.SMEM),
            pl.BlockSpec(memory_space=pltpu.VMEM),
            pl.BlockSpec(memory_space=pltpu.VMEM),
            pl.BlockSpec(memory_space=pl.ANY),
            pl.BlockSpec(memory_space=pl.ANY),
        ],
        out_specs=(pl.BlockSpec(memory_space=pltpu.VMEM), pl.BlockSpec(memory_space=pltpu.VMEM)),
        scratch_shapes=[
            vm(amplitudes.shape, jnp.bfloat16),
            vm(tiles.shape, jnp.bfloat16),
            vm(tiles.shape, jnp.bfloat16),
            vm((PIECES, every // PIECES, TILE, TILE), jnp.bfloat16),
            vm((every + 1, TILE, TILE), jnp.bfloat16),
            vm(first_q, jnp.int16), vm(first_u, jnp.float32), vm(first_q, jnp.int16), vm(first_u, jnp.float32),
            vm(second_q, jnp.int16), vm(second_u, jnp.float32), vm(second_q, jnp.int16), vm(second_u, jnp.float32),
            vm((2, 4, half, TILE), jnp.float32), vm((4, half, TILE), jnp.float32),
            vm(tile_ab.shape, jnp.int32), vm(tile_ab.shape, jnp.int32),
            vm((tiles.shape[0], TILE), jnp.int32), vm((rows_of_table, TILE), jnp.int32),
            pltpu.SMEM((tiles.shape[0], TILE), jnp.int32), pltpu.SMEM((rows_of_table, TILE), jnp.int32),
            dma((3,)), dma((8, PIECES)), dma((8, PIECES)),
            dma((2, 4, 4)), dma((2, 4, 4)), dma((2, 4, 4)), dma((2, 4, 4)),
            dma((2, 4)), dma((2, 4)), dma((2, 4)), dma((2, 4)),
        ],
        compiler_params=pltpu.CompilerParams(
            collective_id=barrier_id, has_side_effects=True, vmem_limit_bytes=60 * 2**20
        ),
    )(slot_tile, tile_ab, tile_cd, amplitudes, tiles)


def shards(
    amplitudes, integral_tiles, tile_cd, tile_ab, slot_tile, residual_in, occ_level, vir_level
):
    operands = (slot_tile, tile_ab, tile_cd, amplitudes, integral_tiles[0])
    by_slot, crowded = ladder(EARLY, 0, *operands)

    def update(value):
        return (residual_in + value) / (occ_level[:, None] - vir_level[None, :])

    return lax.cond(
        crowded[0, 0] > 0.0,
        lambda: update(ladder(LATE, 1, *operands)[0]),
        lambda: update(by_slot),
    )


def solution(mesh):
    in_specs = (
        P("occ", "vir"),
        P("vir", "occ", None, None),
        P(),
        P(),
        P(),
        P("occ", "vir"),
        P("occ"),
        P("vir"),
    )
    out_specs = P("occ", "vir")
    return jax.shard_map(shards, mesh=mesh, in_specs=in_specs, out_specs=out_specs, check_vma=False)
```

time: 94.4 us -> 76.3 us (0.81)
  Pallas kernels: 87.3 us -> 71.3 us
  other arithmetic: 3.4 us -> 1.75 us
  matrix products: 1.02 us -> 0 us
    pallas_call x1, Pallas kernels: 87.3 us -> 71.3 us  [ladder(): pl.pallas_call(functools.partial(kernel, need), out_shape=(jax.ShapeDtype...]
    reshape x3 -> x0, local copies, waits for them, and re-layouts: 1.46 us -> none  [the longest x1 0.69 us: shards(): table = jnp.where(named == 0, count, named - 1).reshape(-1)]
    slice x0 -> x1, local copies, waits for them, and re-layouts: none -> 1.2 us  [shards(): crowded[0, 0] > 0.0]
    dot_general x1 -> x0, matrix products: 1.02 us -> none  [shards(): jnp.dot(match.astype(jnp.float32), of_kind, precision=lax.Precision.HIGHEST)]
    unnamed x6 -> x14, local copies, waits for them, and re-layouts: 0.01 us -> 0.99 us
where the time goes in v3:
time: 76.3 us; the launch traced here: 76 us
  Pallas kernels  71.3 us (93%)
  local copies, waits for them, and re-layouts  2.19 us (3%)
  other arithmetic  1.75 us (2%)
    pallas_call x1, Pallas kernels, ladder(): pl.pallas_call(functools.partial(kernel, need), out_shape=(jax.ShapeDtype...  71.3 us
    div x1, other arithmetic, update(): return (residual_in + value) / (occ_level[:, None] - vir_level[None, :])  1.75 us

profile of v3, /device:TPU:1, one launch (start us, length us, event | category | flops | bytes accessed | tf_op | source)
XLA Modules:
  0.0 76.0 jit_solution(9643782346305862525)
XLA Ops:
  0.0 0.0 copy-start.5
  0.0 0.0 copy-start.4
  0.0 0.0 copy-start.6
  0.0 0.0 copy-start.2
  0.0 0.0 copy-start.3
  0.0 0.0 copy-start
  0.0 71.3 %shard_map.84 = (f32[512,512]{1,0:T(8,128)}, f32[8,128]{1,0:T(8,128)}) custom-call(s32[64]{0:T(128)} %slot_tile.1, s32[16,256]{1,0:T(8,128)} %tile_ab.1, s32[16,256]{1,0:T(8,128)} %tile_cd.1, bf16[512,3072]{1,0:T(8,128)(2,1)} %amp_hbm.1, bf16[32,128,128]{2,1,0:T(8,128)(2,1)} %bitcast.2), custom_call_target="tpu_custom_call" | custom-call | tf_op jit(solution)/shard_map/pallas_call | solution.py:404
  71.4 1.2 %slice.3 = f32[1,1]{1,0:T(1,128)} slice(f32[8,128]{1,0:T(8,128)} %get-tuple-element.47), slice={[0:1], [0:1]} | slice | bytes 8 | tf_op jit(solution)/shard_map/slice | solution.py:450
  73.2 0.0 copy-done.5
  73.2 0.0 copy-done.4
  73.2 0.0 copy-done.6
  73.2 0.0 copy-done.2
  73.3 0.0 copy-done.3
  73.3 0.0 copy-done
  73.3 1.8 %conditional.1 = (f32[512,512]{1,0:T(8,128)S(1)}) conditional(s32[]{:T(128)} %bitcast.1, (f32[512,512]{1,0:T(8,128)}, f32[512,512]{1,0:T(8,128)}, f32[512]{0:T(512)S(1)}, f32[512]{0:T(512)S(1)}) %tuple.24, (s32[64]{0:T(128)S(1)}, s32[16,256]{1,0:T(8,128)S(1)}, s32[16,256]{1,0:T(8,128)S(1)}, bf16[512,3072]{1,0:T(8,128)(2,1)S(1)}, ...), branch_computations={%region_0.0_spmd, %region_1.0_spmd} | conditional | flops 786432 | bytes 3149832 | solution.py:449
  73.3 1.8 %subtract_divide_fusion = f32[512,512]{1,0:T(8,128)S(1)} fusion(f32[512,512]{1,0:T(8,128)} %get-tuple-element.32, f32[512,512]{1,0:T(8,128)} %get-tuple-element.33, f32[512]{0:T(512)S(1)} %get-tuple-element.35, f32[512]{0:T(512)S(1)} %get-tuple-element.34), kind=kLoop, calls=%fused_computation | loop fusion | flops 786432 | bytes 3149824 | tf_op jit(solution)/shard_map/cond/branch_0_fun/div | solution.py:447
  75.1 0.0 copy-start.1
  75.1 1.0 %copy-done.1 = f32[512,512]{1,0:T(8,128)} copy-done((f32[512,512]{1,0:T(8,128)}, f32[512,512]{1,0:T(8,128)S(1)}, u32[]{:S(2)}) %copy-start.1) | copy-done | bytes 1048600
Async XLA Ops:
  0.0 73.2 %copy-start.5 = (f32[512]{0:T(512)S(1)}, f32[512]{0:T(512)}, u32[]{:S(2)}) copy-start(f32[512]{0:T(512)} %param.17) | copy-start | bytes 6148
  0.0 73.2 %copy-start.4 = (f32[512]{0:T(512)S(1)}, f32[512]{0:T(512)}, u32[]{:S(2)}) copy-start(f32[512]{0:T(512)} %param.16) | copy-start | bytes 6148
  0.0 73.2 %copy-start.6 = (s32[64]{0:T(128)S(1)}, s32[64]{0:T(128)}, u32[]{:S(2)}) copy-start(s32[64]{0:T(128)} %slot_tile.1) | copy-start | bytes 772
  0.0 73.2 %copy-start.2 = (s32[16,256]{1,0:T(8,128)S(1)}, s32[16,256]{1,0:T(8,128)}, u32[]{:S(2)}) copy-start(s32[16,256]{1,0:T(8,128)} %tile_ab.1) | copy-start | bytes 49156
  0.0 73.2 %copy-start.3 = (s32[16,256]{1,0:T(8,128)S(1)}, s32[16,256]{1,0:T(8,128)}, u32[]{:S(2)}) copy-start(s32[16,256]{1,0:T(8,128)} %tile_cd.1) | copy-start | bytes 49156
  0.0 73.2 %copy-start = (bf16[512,3072]{1,0:T(8,128)(2,1)S(1)}, bf16[512,3072]{1,0:T(8,128)(2,1)}, u32[]{:S(2)}) copy-start(bf16[512,3072]{1,0:T(8,128)(2,1)} %amp_hbm.1) | copy-start | bytes 9437188
  75.1 1.0 %copy-start.1 = (f32[512,512]{1,0:T(8,128)}, f32[512,512]{1,0:T(8,128)S(1)}, u32[]{:S(2)}) copy-start(f32[512,512]{1,0:T(8,128)S(1)} %get-tuple-element.52) | copy-start | bytes 3145732

commit v4 on v3

--- a/solution.py
+++ b/solution.py
@@ -363,8 +363,6 @@
         for e in (1, 3):
             for copy in second_leg(h, e):
                 copy.wait_recv()
-
-    for h in range(2):
 
         def finish(n, carry):
             span = pl.ds(pl.multiple_of(n * step, step), step)

time: 76.3 us -> 76.2 us (level)
  no operation moved by 1% of the time
where the time goes in v4:
time: 76.2 us; the launch traced here: 76 us
  Pallas kernels  71.3 us (94%)
  local copies, waits for them, and re-layouts  2.19 us (3%)
  other arithmetic  1.75 us (2%)
    pallas_call x1, Pallas kernels, ladder(): pl.pallas_call(functools.partial(kernel, need), out_shape=(jax.ShapeDtype...  71.3 us
    div x1, other arithmetic, update(): return (residual_in + value) / (occ_level[:, None] - vir_level[None, :])  1.75 us

profile of v4, /device:TPU:1, one launch (start us, length us, event | category | flops | bytes accessed | tf_op | source)
XLA Modules:
  0.0 76.0 jit_solution(214348410534930361)
XLA Ops:
  0.0 0.0 copy-start.5
  0.0 0.0 copy-start.4
  0.0 0.0 copy-start.6
  0.0 0.0 copy-start.2
  0.0 0.0 copy-start.3
  0.0 0.0 copy-start
  0.0 71.3 %shard_map.84 = (f32[512,512]{1,0:T(8,128)}, f32[8,128]{1,0:T(8,128)}) custom-call(s32[64]{0:T(128)} %slot_tile.1, s32[16,256]{1,0:T(8,128)} %tile_ab.1, s32[16,256]{1,0:T(8,128)} %tile_cd.1, bf16[512,3072]{1,0:T(8,128)(2,1)} %amp_hbm.1, bf16[32,128,128]{2,1,0:T(8,128)(2,1)} %bitcast.2), custom_call_target="tpu_custom_call" | custom-call | tf_op jit(solution)/shard_map/pallas_call | solution.py:402
  71.4 1.2 %slice.3 = f32[1,1]{1,0:T(1,128)} slice(f32[8,128]{1,0:T(8,128)} %get-tuple-element.47), slice={[0:1], [0:1]} | slice | bytes 8 | tf_op jit(solution)/shard_map/slice | solution.py:448
  73.2 0.0 copy-done.5
  73.2 0.0 copy-done.4
  73.2 0.0 copy-done.6
  73.2 0.0 copy-done.2
  73.3 0.0 copy-done.3
  73.3 0.0 copy-done
  73.3 1.8 %conditional.1 = (f32[512,512]{1,0:T(8,128)S(1)}) conditional(s32[]{:T(128)} %bitcast.1, (f32[512,512]{1,0:T(8,128)}, f32[512,512]{1,0:T(8,128)}, f32[512]{0:T(512)S(1)}, f32[512]{0:T(512)S(1)}) %tuple.24, (s32[64]{0:T(128)S(1)}, s32[16,256]{1,0:T(8,128)S(1)}, s32[16,256]{1,0:T(8,128)S(1)}, bf16[512,3072]{1,0:T(8,128)(2,1)S(1)}, ...), branch_computations={%region_0.0_spmd, %region_1.0_spmd} | conditional | flops 786432 | bytes 3149832 | solution.py:447
  73.3 1.8 %subtract_divide_fusion = f32[512,512]{1,0:T(8,128)S(1)} fusion(f32[512,512]{1,0:T(8,128)} %get-tuple-element.32, f32[512,512]{1,0:T(8,128)} %get-tuple-element.33, f32[512]{0:T(512)S(1)} %get-tuple-element.35, f32[512]{0:T(512)S(1)} %get-tuple-element.34), kind=kLoop, calls=%fused_computation | loop fusion | flops 786432 | bytes 3149824 | tf_op jit(solution)/shard_map/cond/branch_0_fun/div | solution.py:445
  75.0 0.0 copy-start.1
  75.1 1.0 %copy-done.1 = f32[512,512]{1,0:T(8,128)} copy-done((f32[512,512]{1,0:T(8,128)}, f32[512,512]{1,0:T(8,128)S(1)}, u32[]{:S(2)}) %copy-start.1) | copy-done | bytes 1048600
Async XLA Ops:
  0.0 73.2 %copy-start.5 = (f32[512]{0:T(512)S(1)}, f32[512]{0:T(512)}, u32[]{:S(2)}) copy-start(f32[512]{0:T(512)} %param.17) | copy-start | bytes 6148
  0.0 73.2 %copy-start.4 = (f32[512]{0:T(512)S(1)}, f32[512]{0:T(512)}, u32[]{:S(2)}) copy-start(f32[512]{0:T(512)} %param.16) | copy-start | bytes 6148
  0.0 73.2 %copy-start.6 = (s32[64]{0:T(128)S(1)}, s32[64]{0:T(128)}, u32[]{:S(2)}) copy-start(s32[64]{0:T(128)} %slot_tile.1) | copy-start | bytes 772
  0.0 73.2 %copy-start.2 = (s32[16,256]{1,0:T(8,128)S(1)}, s32[16,256]{1,0:T(8,128)}, u32[]{:S(2)}) copy-start(s32[16,256]{1,0:T(8,128)} %tile_ab.1) | copy-start | bytes 49156
  0.0 73.2 %copy-start.3 = (s32[16,256]{1,0:T(8,128)S(1)}, s32[16,256]{1,0:T(8,128)}, u32[]{:S(2)}) copy-start(s32[16,256]{1,0:T(8,128)} %tile_cd.1) | copy-start | bytes 49156
  0.0 73.2 %copy-start = (bf16[512,3072]{1,0:T(8,128)(2,1)S(1)}, bf16[512,3072]{1,0:T(8,128)(2,1)}, u32[]{:S(2)}) copy-start(bf16[512,3072]{1,0:T(8,128)(2,1)} %amp_hbm.1) | copy-start | bytes 9437188
  75.0 1.0 %copy-start.1 = (f32[512,512]{1,0:T(8,128)}, f32[512,512]{1,0:T(8,128)S(1)}, u32[]{:S(2)}) copy-start(f32[512,512]{1,0:T(8,128)S(1)} %get-tuple-element.52) | copy-start | bytes 3145732
